TPU v7x, 512 devices: a whole 4x4x16 slice. The times are simulated.
512 devices in a mesh: dom: 128 (over z, y, core), src: 4 (over x).
Axes of the slice: x: 4, y: 4, z: 16, core: 2. Of those that a mesh axis runs over, the one named last changes fastest.
Arguments:
- features: bfloat16 [524288, 256], P(('dom', 'src')), may hold values from -6 to 6
- cotangent: bfloat16 [524288, 256], P(('dom', 'src')), may hold values from -6 to 6
- w_self: bfloat16 [256, 256], replicated, may hold values from -0.375 to 0.375
- w_neigh: bfloat16 [256, 256], replicated, may hold values from -0.375 to 0.375
- bias: bfloat16 [256], replicated, may hold values from -3 to 3
- send_rows: int32 [128, 4, 128, 8], P('dom', 'src'), may hold values from -1 to 1023, as said below
- edge_src: int32 [128, 4, 8192], P('dom', 'src'), may hold values from 0 to 2047, as said below
- edge_dst: int32 [128, 4, 8192], P('dom', 'src'), may hold values from 0 to 4095
- tile_count: int32 [128, 4], P('dom', 'src'), may hold values from 16 to 64, as said below
Outputs:
- activations: bfloat16 [524288, 256], P(('dom', 'src'))
- feature_grad: float32 [524288, 256], P(('dom', 'src'))
Inputs may be any that keep to these rules, and one draw needn't show every extreme that they name: `send_rows`: slots of a list are filled from the first one; some list of every owner is full; an account's own part sends it nothing. `edge_src`: every edge refers to a local row or to a filled slot. Edge slots after the first tile_count * 128 are ignored.
All inputs are finite; a program needn't handle non-finite values.
Results may differ from a plain program's by a relative error of at most 0.009.
Values may be sent and summed in bfloat16 or wider, within the bound.
No kernel may reach another device: no remote copies, remote signals or barrier semaphores. Data moves between devices by JAX's collectives and lax.ppermute only.
A program may use at most 64 MiB of HBM per device.

v0:
```python
import jax
import jax.numpy as jnp
from jax import lax
from jax.sharding import PartitionSpec as P


def local(features, cotangent, w_self, w_neigh, bias, send_rows, edge_src, edge_dst, tile_count):
    node_rows = features.shape[0]
    feature_width = features.shape[1]
    peer_total = lax.axis_size("dom")
    senders = send_rows[0, 0]
    capacity = senders.shape[1]
    halo_total = peer_total * capacity
    sources = edge_src[0, 0]
    targets = edge_dst[0, 0]
    edge_total = sources.shape[0]
    part_total = node_rows * lax.axis_size("src")
    active = jnp.arange(edge_total) // 128 < tile_count[0, 0]
    filled = senders >= 0
    zero_half = jnp.zeros((), jnp.bfloat16)
    picked = jnp.where(filled[:, :, None], features[jnp.maximum(senders, 0)], zero_half)
    counts = jnp.zeros((part_total,), jnp.float32).at[targets].add(active.astype(jnp.float32))
    degree_all = lax.psum(counts, "src")
    inverse_all = 1.0 / jnp.maximum(degree_all, 1.0)
    inverse = lax.dynamic_slice_in_dim(inverse_all, lax.axis_index("src") * node_rows, node_rows)
    remote = lax.all_to_all(picked, "dom", split_axis=0, concat_axis=0, tiled=True).reshape(
        halo_total, feature_width
    )
    table = jnp.concatenate([features, remote], axis=0)
    taken = jnp.where(active[:, None], table[sources], zero_half)
    partial_value = (
        jnp.zeros((part_total, feature_width), jnp.float32)
        .at[targets]
        .add(taken.astype(jnp.float32))
    )
    totals = lax.psum_scatter(
        partial_value.astype(jnp.bfloat16), "src", scatter_dimension=0, tiled=True
    ).astype(jnp.float32)
    neighbour_mean = (totals * inverse[:, None]).astype(jnp.bfloat16)
    preact = (
        jnp.dot(features, w_self, preferred_element_type=jnp.float32)
        + jnp.dot(neighbour_mean, w_neigh, preferred_element_type=jnp.float32)
        + bias.astype(jnp.float32)
    )
    sigma = jax.nn.sigmoid(preact)
    outputs = (preact * sigma).astype(jnp.bfloat16)
    slope = sigma * (1.0 + preact * (1.0 - sigma))
    upstream = (cotangent.astype(jnp.float32) * slope).astype(jnp.bfloat16)
    grad_own = jnp.dot(upstream, w_self.T, preferred_element_type=jnp.float32)
    scaled = (
        jnp.dot(upstream, w_neigh.T, preferred_element_type=jnp.float32) * inverse[:, None]
    ).astype(jnp.bfloat16)
    spread = lax.all_gather(scaled, "src", axis=0, tiled=True)
    contrib = jnp.where(active[:, None], spread[targets], zero_half).astype(jnp.float32)
    grad_table = (
        jnp.zeros((node_rows + halo_total, feature_width), jnp.float32).at[sources].add(contrib)
    )
    remote_grad = grad_table[node_rows:]
    local_grad = grad_table[:node_rows]
    returned = lax.all_to_all(
        remote_grad.reshape(peer_total, capacity, feature_width).astype(jnp.bfloat16),
        "dom",
        split_axis=0,
        concat_axis=0,
        tiled=True,
    ).astype(jnp.float32)
    back_rows = jnp.where(filled, senders, node_rows)
    incoming = (
        jnp.zeros((node_rows, feature_width), jnp.float32).at[back_rows].add(returned, mode="drop")
    )
    return (outputs, grad_own + local_grad + incoming)


def solution(mesh):
    placed = (
        P(("dom", "src"), None),
        P(("dom", "src"), None),
        P(),
        P(),
        P(),
        P("dom", "src", None, None),
        P("dom", "src", None),
        P("dom", "src", None),
        P("dom", "src"),
    )
    return jax.shard_map(
        local,
        mesh=mesh,
        in_specs=placed,
        out_specs=(P(("dom", "src"), None), P(("dom", "src"), None)),
        check_vma=False,
    )
```

profile of v0, /device:TPU:33, one launch (start us, length us, event | category | flops | bytes accessed | tf_op | source)
XLA Modules:
  0.0 406.9 jit_solution(14900899894254317384)
XLA Ops:
  7.2 0.0 copy-start
  7.2 0.0 copy-start.1
  7.2 0.0 copy-start.3
  7.2 0.0 copy-start.4
  7.2 0.8 compare_select_fusion.2
  8.0 0.7 compare_bitcast_fusion
  8.7 0.1 copy.13
  8.8 0.1 reshape.127
  8.9 0.1 copy.12
  9.0 4.6 %gather_fusion = bf16[1024,256]{1,0:T(8,128)(2,1)S(1)} fusion(bf16[1024,256]{1,0:T(8,128)(2,1)} %param.9, s32[1024]{0:T(1024)S(1)} %broadcast_clamp_fusion.2), kind=kCustom, calls=%fused_computation | custom fusion | bytes 1052672 | tf_op jit(solution)/shard_map/gather | solution.py:21
  13.6 1.0 bitcast_select_fusion
  14.6 19.5 %all-to-all-start = ((bf16[128,8,256]{2,1,0:T(8,128)(2,1)}), bf16[128,8,256]{2,1,0:T(8,128)(2,1)S(1)}, u32[]{:S(2)}, u32[]{:S(2)}) async-start(bf16[128,8,256]{2,1,0:T(8,128)(2,1)} %bitcast_select_fusion), calls=%async_computation | async-start | bytes 1048576 | tf_op jit(solution)/shard_map/all_to_all | solution.py:26
  34.1 0.0 reduce-scatter.2.cloned.1.call-start
  34.8 0.0 copy-done.3
  34.8 0.0 copy-done.4
  34.9 32.7 %all-to-all-done = bf16[128,8,256]{2,1,0:T(8,128)(2,1)S(1)} async-done(((bf16[128,8,256]{2,1,0:T(8,128)(2,1)}), bf16[128,8,256]{2,1,0:T(8,128)(2,1)S(1)}, u32[]{:S(2)}, u32[]{:S(2)}) %all-to-all-start) | async-done | bytes 524320 | tf_op jit(solution)/shard_map/all_to_all | solution.py:26
  67.6 0.0 copy-done.1
  67.6 0.1 pad_maximum_fusion
  67.7 76.8 %scatter_custom_fusion = f32[4096,256]{1,0:T(8,128)} fusion(s32[8192]{0:T(1024)S(1)} %bitcast.39, pred[8192]{0:T(1024)(128)(4,1)S(1)} %fusion.19, bf16[]{:T(256)} %constant.41.clone.1, f32[]{:T(128)} %constant.14.clone.1, bf16[2048,256]{1,0:T(8,128)(2,1)S(1)} %pad_maximum_fusion, s32[8192]{0:T(1024)S(1)} %broadcast_clamp_fusion.1), kind=kCustom, calls=%fused_computation.9 | custom fusion | flops 6291456 | bytes 5283846 | tf_op jit(solution)/shard_map/scatter-add | solution.py:34
  144.6 0.0 copy-start.6
  144.6 0.0 copy-start.2
  144.6 0.0 copy-start.5
  144.6 3.8 convert_element_type.41
  148.3 0.0 reduce-scatter.2.cloned.1.call-update
  148.4 0.0 all-gather.2.cloned.1.call-start
  148.4 43.2 %scatter_custom_fusion.1 = f32[4096]{0:T(1024)S(1)} fusion(s32[8192]{0:T(1024)S(1)} %bitcast.40, f32[8192]{0:T(1024)S(1)} %fusion.25, f32[]{:T(128)} %constant.14.clone.1), kind=kCustom, calls=%fused_computation.50 | custom fusion | flops 8192 | bytes 16388 | tf_op jit(solution)/shard_map/scatter-add | solution.py:22
  191.7 0.0 copy-done.6
  191.7 13.2 %psum.7 = f32[4096]{0:T(1024)S(1)} all-reduce(f32[4096]{0:T(1024)S(1)} %scatter_custom_fusion.1), channel_id=1, replica_groups=mesh['dom'=128,'src'=4] {'src'}, use_global_device_ids=true, to_apply=%region_3.4 | all-reduce | flops 4096 | bytes 32768 | tf_op jit(solution)/shard_map/psum | solution.py:23
  204.8 0.0 copy-done.2
  204.8 0.3 fusion.29
  205.1 0.0 reduce-scatter.2.cloned.1.call-done
  205.2 0.0 copy-done
  205.2 0.0 copy-done.5
  205.2 2.6 multiply_convert_fusion
  207.8 1.1 fusion.12
  208.9 0.0 all-gather.2.cloned.1.call-update
  208.9 31.2 %all-gather.2.cloned.1.call-done = bf16[4096,256]{1,0:T(8,128)(2,1)} async-done(((bf16[1024,256]{1,0:T(8,128)(2,1)}), bf16[4096,256]{1,0:T(8,128)(2,1)}) %all-gather.2.cloned.1.call-update) | async-done | bytes 2097168 | tf_op jit(solution)/shard_map/all_gather | solution.py:53
  240.1 100.4 %scatter_custom_fusion.2 = f32[2048,256]{1,0:T(8,128)S(1)} fusion(s32[8192]{0:T(1024)S(1)} %bitcast.38, pred[8192]{0:T(1024)(128)(4,1)S(1)} %fusion.19, bf16[]{:T(256)} %constant.41.clone.1, f32[]{:T(128)} %constant.14.clone.1, bf16[4096,256]{1,0:T(8,128)(2,1)} %all-gather.2.cloned.1.call-done, s32[8192]{0:T(1024)S(1)} %broadcast_clamp_fusion), kind=kCustom, calls=%fused_computation.7 | custom fusion | flops 6291456 | bytes 4235270 | tf_op jit(solution)/shard_map/scatter-add | solution.py:56
  340.5 0.8 fusion.16
  341.4 16.8 %all-to-all-start.1 = ((bf16[128,8,256]{2,1,0:T(8,128)(2,1)}), bf16[128,8,256]{2,1,0:T(8,128)(2,1)S(1)}, u32[]{:S(2)}, u32[]{:S(2)}) async-start(bf16[128,8,256]{2,1,0:T(8,128)(2,1)} %fusion.16), calls=%async_computation.2 | async-start | bytes 1048576 | tf_op jit(solution)/shard_map/all_to_all | solution.py:60
  358.2 0.1 copy.14
  358.3 0.1 reshape.175
  358.4 1.3 convolution_add_fusion
  359.7 32.1 %all-to-all-done.1 = bf16[128,8,256]{2,1,0:T(8,128)(2,1)S(1)} async-done(((bf16[128,8,256]{2,1,0:T(8,128)(2,1)}), bf16[128,8,256]{2,1,0:T(8,128)(2,1)S(1)}, u32[]{:S(2)}, u32[]{:S(2)}) %all-to-all-start.1) | async-done | bytes 524320 | tf_op jit(solution)/shard_map/all_to_all | solution.py:60
  391.8 8.3 %scatter_custom_fusion.3 = f32[1024,256]{1,0:T(8,128)} fusion(f32[1024,256]{1,0:T(8,128)} %convolution_add_fusion, s32[1024]{0:T(1024)S(1)} %reshape.175, bf16[128,8,256]{2,1,0:T(8,128)(2,1)S(1)} %all-to-all-done.1), kind=kCustom, calls=%fused_computation.25 | custom fusion | flops 524288 | bytes 1572864 | tf_op jit(solution)/shard_map/scatter-add | solution.py:69
  (9 shorter events, 0.1 us)
Async XLA Ops:
  7.2 198.0 %copy-start = (bf16[256,256]{1,0:T(8,128)(2,1)S(1)}, bf16[256,256]{1,0:T(8,128)(2,1)}, u32[]{:S(2)}) copy-start(bf16[256,256]{1,0:T(8,128)(2,1)} %param.12) | copy-start | bytes 393220
  7.2 60.5 %copy-start.1 = (bf16[1024,256]{1,0:T(8,128)(2,1)S(1)}, bf16[1024,256]{1,0:T(8,128)(2,1)}, u32[]{:S(2)}) copy-start(bf16[1024,256]{1,0:T(8,128)(2,1)} %param.9) | copy-start | bytes 1572868
  7.2 27.6 %copy-start.3 = (s32[1,1,8192]{2,1,0:T(1,128)S(1)}, s32[1,1,8192]{2,1,0:T(1,128)}, u32[]{:S(2)}) copy-start(s32[1,1,8192]{2,1,0:T(1,128)} %param.15) | copy-start | bytes 98308
  7.2 27.6 %copy-start.4 = (s32[1,1,8192]{2,1,0:T(1,128)S(1)}, s32[1,1,8192]{2,1,0:T(1,128)}, u32[]{:S(2)}) copy-start(s32[1,1,8192]{2,1,0:T(1,128)} %param.16) | copy-start | bytes 98308
  14.6 53.1 %all-to-all-start = ((bf16[128,8,256]{2,1,0:T(8,128)(2,1)}), bf16[128,8,256]{2,1,0:T(8,128)(2,1)S(1)}, u32[]{:S(2)}, u32[]{:S(2)}) async-start(bf16[128,8,256]{2,1,0:T(8,128)(2,1)} %bitcast_select_fusion), calls=%async_computation | async-start | bytes 1048576 | tf_op jit(solution)/shard_map/all_to_all | solution.py:26
  34.1 171.1 %reduce-scatter.2.cloned.1.call-start = ((), (), s32[]{:S(2)}) async-start(), calls=%async_computation.3 | async-start | bytes 2621440 | tf_op jit(solution)/shard_map/reduce_scatter | solution.py:36
  144.6 47.1 %copy-start.6 = (bf16[256]{0:T(256)(128)(2,1)S(1)}, bf16[256]{0:T(256)(128)(2,1)}, u32[]{:S(2)}) copy-start(bf16[256]{0:T(256)(128)(2,1)} %param.13) | copy-start | bytes 1540
  144.6 60.3 %copy-start.2 = (bf16[256,256]{1,0:T(8,128)(2,1)S(1)}, bf16[256,256]{1,0:T(8,128)(2,1)}, u32[]{:S(2)}) copy-start(bf16[256,256]{1,0:T(8,128)(2,1)} %param.11) | copy-start | bytes 393220
  144.6 60.6 %copy-start.5 = (bf16[1024,256]{1,0:T(8,128)(2,1)S(1)}, bf16[1024,256]{1,0:T(8,128)(2,1)}, u32[]{:S(2)}) copy-start(bf16[1024,256]{1,0:T(8,128)(2,1)} %param.10) | copy-start | bytes 1572868
  148.4 91.8 %all-gather.2.cloned.1.call-start = ((), (), s32[]{:S(2)}) async-start(), calls=%async_computation.4 | async-start | bytes 2621440 | tf_op jit(solution)/shard_map/all_gather | solution.py:53
  341.4 50.4 %all-to-all-start.1 = ((bf16[128,8,256]{2,1,0:T(8,128)(2,1)}), bf16[128,8,256]{2,1,0:T(8,128)(2,1)S(1)}, u32[]{:S(2)}, u32[]{:S(2)}) async-start(bf16[128,8,256]{2,1,0:T(8,128)(2,1)} %fusion.16), calls=%async_computation.2 | async-start | bytes 1048576 | tf_op jit(solution)/shard_map/all_to_all | solution.py:60
Sparse Core Ops, SparseCore 0:
  148.5 28.3 reduce-scatter.1
  209.0 31.0 all-gather.1
where the time goes:
time: 408 us; the launch traced here: 407 us
  other arithmetic  235 us (58%)
  waiting for transfers between devices  96.1 us (24%)
  starting transfers between devices  36.4 us (9%)
  between operations  14.9 us (4%)
  blocking collectives  13.2 us (3%)
  local copies, waits for them, and re-layouts  5.95 us (1%)
  matrix products  5.3 us (1%)
    scatter-add x1, other arithmetic, local(): jnp.zeros((node_rows + halo_total, feature_width), jnp.float32).at[sources]  100 us
    scatter-add x1, other arithmetic, local(): partial_value = jnp.zeros((part_total, feature_width), jnp.float32).at[ta...  76.8 us
    scatter-add x1, other arithmetic, local(): jnp.zeros((part_total,), jnp.float32).at[targets]  43.2 us
    all_to_all x1, waiting for transfers between devices, local(): lax.all_to_all(picked, 'dom', split_axis=0, concat_axis=0, tiled=True)  32.7 us
    all_to_all x1, waiting for transfers between devices, local(): lax.all_to_all(remote_grad.reshape(peer_total, capacity, feature_width).a...  32.1 us
    all_gather x1, waiting for transfers between devices, local(): spread = lax.all_gather(scaled, 'src', axis=0, tiled=True)  31.2 us
    all_to_all x1, starting transfers between devices, local(): lax.all_to_all(picked, 'dom', split_axis=0, concat_axis=0, tiled=True)  19.5 us
    all_to_all x1, starting transfers between devices, local(): lax.all_to_all(remote_grad.reshape(peer_total, capacity, feature_width).a...  16.8 us
  transfers between devices with their start and end apart: 4, of which 3 were waited for; matrix products, arithmetic and copies ran while one was open for 11% of the time, Pallas kernels for 0%

commit v1 on v0

--- a/solution.py
+++ b/solution.py
@@ -2,6 +2,7 @@
 import jax.numpy as jnp
 from jax import lax
 from jax.sharding import PartitionSpec as P
+from jax.lax import all_to_all, axis_size
 
 
 def local(features, cotangent, w_self, w_neigh, bias, send_rows, edge_src, edge_dst, tile_count):
@@ -50,7 +51,10 @@
     scaled = (
         jnp.dot(upstream, w_neigh.T, preferred_element_type=jnp.float32) * inverse[:, None]
     ).astype(jnp.bfloat16)
-    spread = lax.all_gather(scaled, "src", axis=0, tiled=True)
+    spread = jnp.concatenate(
+        all_to_all(jnp.stack([scaled] * axis_size("src")), "src", split_axis=0, concat_axis=0),
+        axis=0,
+    )
     contrib = jnp.where(active[:, None], spread[targets], zero_half).astype(jnp.float32)
     grad_table = (
         jnp.zeros((node_rows + halo_total, feature_width), jnp.float32).at[sources].add(contrib)

time: 408 us -> 373 us (0.914)
  other arithmetic: 235 us -> 209 us
  waiting for transfers between devices: 96.1 us -> 87.2 us
    all_gather x1 -> x0, waiting for transfers between devices: 31.2 us -> none  [local(): spread = lax.all_gather(scaled, 'src', axis=0, tiled=True)]
    scatter-add x1, other arithmetic: 100 us -> 76.1 us  [local(): jnp.zeros((node_rows + halo_total, feature_width), jnp.float32).at[sources]]
    all_to_all x0 -> x1, waiting for transfers between devices: none -> 22.6 us  [local(): all_to_all(jnp.stack([scaled] * axis_size('src')), 'src', split_axis=0, c...]
    all_to_all x1, starting transfers between devices: 16.8 us -> 10.1 us  [local(): lax.all_to_all(remote_grad.reshape(peer_total, capacity, feature_width).a...]
  transfers between devices with their start and end apart: 4 -> 4, of which waited for: 3 -> 3; matrix products, arithmetic and copies ran while one was open for 11% -> 12% of each run, Pallas kernels for 0% -> 0%
where the time goes in v1:
time: 373 us; the launch traced here: 372 us
  other arithmetic  209 us (56%)
  waiting for transfers between devices  87.2 us (23%)
  starting transfers between devices  33.4 us (9%)
  between operations  14.9 us (4%)
  blocking collectives  13.1 us (4%)
  local copies, waits for them, and re-layouts  9.63 us (3%)
  matrix products  4.75 us (1%)
    scatter-add x1, other arithmetic, local(): partial_value = jnp.zeros((part_total, feature_width), jnp.float32).at[ta...  76.8 us
    scatter-add x1, other arithmetic, local(): jnp.zeros((node_rows + halo_total, feature_width), jnp.float32).at[sources]  76.1 us
    scatter-add x1, other arithmetic, local(): jnp.zeros((part_total,), jnp.float32).at[targets]  43.2 us
    all_to_all x1, waiting for transfers between devices, local(): lax.all_to_all(picked, 'dom', split_axis=0, concat_axis=0, tiled=True)  32.7 us
    all_to_all x1, waiting for transfers between devices, local(): lax.all_to_all(remote_grad.reshape(peer_total, capacity, feature_width).a...  31.8 us
    all_to_all x1, waiting for transfers between devices, local(): all_to_all(jnp.stack([scaled] * axis_size('src')), 'src', split_axis=0, c...  22.6 us
    all_to_all x1, starting transfers between devices, local(): lax.all_to_all(picked, 'dom', split_axis=0, concat_axis=0, tiled=True)  19.5 us
    psum x1, blocking collectives, local(): degree_all = lax.psum(counts, 'src')  13.1 us
  transfers between devices with their start and end apart: 4, of which 3 were waited for; matrix products, arithmetic and copies ran while one was open for 12% of the time, Pallas kernels for 0%

profile of v1, /device:TPU:33, one launch (start us, length us, event | category | flops | bytes accessed | tf_op | source)
XLA Modules:
  0.0 372.0 jit_solution(9073737643823150255)
XLA Ops:
  7.2 0.0 copy-start
  7.2 0.0 copy-start.1
  7.2 0.0 copy-start.4
  7.2 0.0 copy-start.5
  7.2 0.8 compare_select_fusion.2
  8.0 0.7 compare_bitcast_fusion
  8.7 0.1 copy.13
  8.8 0.1 reshape.133
  8.9 0.1 copy.12
  9.0 4.6 %gather_fusion = bf16[1024,256]{1,0:T(8,128)(2,1)S(1)} fusion(bf16[1024,256]{1,0:T(8,128)(2,1)} %param.9, s32[1024]{0:T(1024)S(1)} %broadcast_clamp_fusion.2), kind=kCustom, calls=%fused_computation | custom fusion | bytes 1052672 | tf_op jit(solution)/shard_map/gather | solution.py:22
  13.6 1.0 bitcast_select_fusion
  14.6 19.5 %all-to-all-start = ((bf16[128,8,256]{2,1,0:T(8,128)(2,1)}), bf16[128,8,256]{2,1,0:T(8,128)(2,1)S(1)}, u32[]{:S(2)}, u32[]{:S(2)}) async-start(bf16[128,8,256]{2,1,0:T(8,128)(2,1)} %bitcast_select_fusion), calls=%async_computation | async-start | bytes 1048576 | tf_op jit(solution)/shard_map/all_to_all | solution.py:27
  34.1 0.0 reduce-scatter.2.cloned.1.call-start
  34.8 0.0 copy-done.4
  34.8 0.0 copy-done.5
  34.9 32.7 %all-to-all-done = bf16[128,8,256]{2,1,0:T(8,128)(2,1)S(1)} async-done(((bf16[128,8,256]{2,1,0:T(8,128)(2,1)}), bf16[128,8,256]{2,1,0:T(8,128)(2,1)S(1)}, u32[]{:S(2)}, u32[]{:S(2)}) %all-to-all-start) | async-done | bytes 524320 | tf_op jit(solution)/shard_map/all_to_all | solution.py:27
  67.6 0.0 copy-done.1
  67.6 0.1 pad_maximum_fusion
  67.7 76.8 %scatter_custom_fusion = f32[4096,256]{1,0:T(8,128)} fusion(s32[8192]{0:T(1024)S(1)} %bitcast.41, pred[8192]{0:T(1024)(128)(4,1)S(1)} %fusion.19, bf16[]{:T(256)} %constant.41.clone.1, f32[]{:T(128)} %constant.14.clone.1, bf16[2048,256]{1,0:T(8,128)(2,1)S(1)} %pad_maximum_fusion, s32[8192]{0:T(1024)S(1)} %broadcast_clamp_fusion.1), kind=kCustom, calls=%fused_computation.9 | custom fusion | flops 6291456 | bytes 5283846 | tf_op jit(solution)/shard_map/scatter-add | solution.py:35
  144.6 0.0 copy-start.7
  144.6 0.0 copy-start.3
  144.6 0.0 copy-start.6
  144.6 3.8 %convert_element_type.41 = bf16[4096,256]{1,0:T(8,128)(2,1)} convert(f32[4096,256]{1,0:T(8,128)} %scatter_custom_fusion) | non-fusion elementwise | flops 1048576 | bytes 6291456 | tf_op jit(solution)/shard_map/convert_element_type | solution.py:38
  148.3 0.0 reduce-scatter.2.cloned.1.call-update
  148.4 43.2 %scatter_custom_fusion.1 = f32[4096]{0:T(1024)S(1)} fusion(s32[8192]{0:T(1024)S(1)} %bitcast.42, f32[8192]{0:T(1024)S(1)} %fusion.25, f32[]{:T(128)} %constant.14.clone.1), kind=kCustom, calls=%fused_computation.50 | custom fusion | flops 8192 | bytes 16388 | tf_op jit(solution)/shard_map/scatter-add | solution.py:23
  191.6 0.0 copy-done.7
  191.6 13.1 %psum.7 = f32[4096]{0:T(1024)S(1)} all-reduce(f32[4096]{0:T(1024)S(1)} %scatter_custom_fusion.1), channel_id=1, replica_groups=mesh['dom'=128,'src'=4] {'src'}, use_global_device_ids=true, to_apply=%region_3.4 | all-reduce | flops 4096 | bytes 32768 | tf_op jit(solution)/shard_map/psum | solution.py:24
  204.8 0.0 copy-done.3
  204.8 0.3 fusion.29
  205.1 0.0 reduce-scatter.2.cloned.1.call-done
  205.1 0.0 copy-done
  205.1 0.0 copy-done.6
  205.1 2.6 multiply_convert_fusion
  207.7 0.3 fusion.12
  208.0 1.5 stack.2
  209.5 3.8 %all-to-all-start.1 = ((bf16[4,1024,256]{2,1,0:T(8,128)(2,1)}), bf16[4,1024,256]{2,1,0:T(8,128)(2,1)S(1)}, u32[]{:S(2)}, u32[]{:S(2)}) async-start(bf16[4,1024,256]{2,1,0:T(8,128)(2,1)} %stack.2), calls=%async_computation.2 | async-start | bytes 4194304 | tf_op jit(solution)/shard_map/all_to_all | solution.py:55
  213.3 22.6 %all-to-all-done.1 = bf16[4,1024,256]{2,1,0:T(8,128)(2,1)S(1)} async-done(((bf16[4,1024,256]{2,1,0:T(8,128)(2,1)}), bf16[4,1024,256]{2,1,0:T(8,128)(2,1)S(1)}, u32[]{:S(2)}, u32[]{:S(2)}) %all-to-all-start.1) | async-done | bytes 2097184 | tf_op jit(solution)/shard_map/all_to_all | solution.py:55
  235.9 76.1 %scatter_custom_fusion.2 = f32[2048,256]{1,0:T(8,128)} fusion(s32[8192]{0:T(1024)S(1)} %bitcast.40, pred[8192]{0:T(1024)(128)(4,1)S(1)} %fusion.19, bf16[]{:T(256)} %constant.41.clone.1, f32[]{:T(128)} %constant.14.clone.1, bf16[4096,256]{1,0:T(8,128)(2,1)S(1)} %bitcast.37, s32[8192]{0:T(1024)S(1)} %broadcast_clamp_fusion), kind=kCustom, calls=%fused_computation.7 | custom fusion | flops 6291456 | bytes 4235270 | tf_op jit(solution)/shard_map/scatter-add | solution.py:60
  312.0 2.1 fusion.16
  314.0 10.1 %all-to-all-start.2 = ((bf16[128,8,256]{2,1,0:T(8,128)(2,1)}), bf16[128,8,256]{2,1,0:T(8,128)(2,1)S(1)}, u32[]{:S(2)}, u32[]{:S(2)}) async-start(bf16[128,8,256]{2,1,0:T(8,128)(2,1)} %fusion.16), calls=%async_computation.3 | async-start | bytes 1048576 | tf_op jit(solution)/shard_map/all_to_all | solution.py:64
  324.1 0.1 copy.14
  324.2 0.1 reshape.181
  324.3 1.6 convolution_add_fusion
  325.9 31.8 %all-to-all-done.2 = bf16[128,8,256]{2,1,0:T(8,128)(2,1)S(1)} async-done(((bf16[128,8,256]{2,1,0:T(8,128)(2,1)}), bf16[128,8,256]{2,1,0:T(8,128)(2,1)S(1)}, u32[]{:S(2)}, u32[]{:S(2)}) %all-to-all-start.2) | async-done | bytes 524320 | tf_op jit(solution)/shard_map/all_to_all | solution.py:64
  357.7 6.5 %scatter_custom_fusion.3 = f32[1024,256]{1,0:T(8,128)S(1)} fusion(f32[1024,256]{1,0:T(8,128)S(1)} %convolution_add_fusion, s32[1024]{0:T(1024)S(1)} %reshape.181, bf16[128,8,256]{2,1,0:T(8,128)(2,1)S(1)} %all-to-all-done.2), kind=kCustom, calls=%fused_computation.25 | custom fusion | flops 524288 | bytes 1572864 | tf_op jit(solution)/shard_map/scatter-add | solution.py:73
  364.2 0.0 copy-start.2
  364.2 1.0 copy-done.2
  (9 shorter events, 0.1 us)
Async XLA Ops:
  7.2 197.9 %copy-start = (bf16[256,256]{1,0:T(8,128)(2,1)S(1)}, bf16[256,256]{1,0:T(8,128)(2,1)}, u32[]{:S(2)}) copy-start(bf16[256,256]{1,0:T(8,128)(2,1)} %param.12) | copy-start | bytes 393220
  7.2 60.5 %copy-start.1 = (bf16[1024,256]{1,0:T(8,128)(2,1)S(1)}, bf16[1024,256]{1,0:T(8,128)(2,1)}, u32[]{:S(2)}) copy-start(bf16[1024,256]{1,0:T(8,128)(2,1)} %param.9) | copy-start | bytes 1572868
  7.2 27.6 %copy-start.4 = (s32[1,1,8192]{2,1,0:T(1,128)S(1)}, s32[1,1,8192]{2,1,0:T(1,128)}, u32[]{:S(2)}) copy-start(s32[1,1,8192]{2,1,0:T(1,128)} %param.15) | copy-start | bytes 98308
  7.2 27.6 %copy-start.5 = (s32[1,1,8192]{2,1,0:T(1,128)S(1)}, s32[1,1,8192]{2,1,0:T(1,128)}, u32[]{:S(2)}) copy-start(s32[1,1,8192]{2,1,0:T(1,128)} %param.16) | copy-start | bytes 98308
  14.6 53.1 %all-to-all-start = ((bf16[128,8,256]{2,1,0:T(8,128)(2,1)}), bf16[128,8,256]{2,1,0:T(8,128)(2,1)S(1)}, u32[]{:S(2)}, u32[]{:S(2)}) async-start(bf16[128,8,256]{2,1,0:T(8,128)(2,1)} %bitcast_select_fusion), calls=%async_computation | async-start | bytes 1048576 | tf_op jit(solution)/shard_map/all_to_all | solution.py:27
  34.1 171.0 %reduce-scatter.2.cloned.1.call-start = ((), (), s32[]{:S(2)}) async-start(), calls=%async_computation.4 | async-start | bytes 2621440 | tf_op jit(solution)/shard_map/reduce_scatter | solution.py:37
  144.6 47.0 %copy-start.7 = (bf16[256]{0:T(256)(128)(2,1)S(1)}, bf16[256]{0:T(256)(128)(2,1)}, u32[]{:S(2)}) copy-start(bf16[256]{0:T(256)(128)(2,1)} %param.13) | copy-start | bytes 1540
  144.6 60.2 %copy-start.3 = (bf16[256,256]{1,0:T(8,128)(2,1)S(1)}, bf16[256,256]{1,0:T(8,128)(2,1)}, u32[]{:S(2)}) copy-start(bf16[256,256]{1,0:T(8,128)(2,1)} %param.11) | copy-start | bytes 393220
  144.6 60.5 %copy-start.6 = (bf16[1024,256]{1,0:T(8,128)(2,1)S(1)}, bf16[1024,256]{1,0:T(8,128)(2,1)}, u32[]{:S(2)}) copy-start(bf16[1024,256]{1,0:T(8,128)(2,1)} %param.10) | copy-start | bytes 1572868
  209.5 26.4 %all-to-all-start.1 = ((bf16[4,1024,256]{2,1,0:T(8,128)(2,1)}), bf16[4,1024,256]{2,1,0:T(8,128)(2,1)S(1)}, u32[]{:S(2)}, u32[]{:S(2)}) async-start(bf16[4,1024,256]{2,1,0:T(8,128)(2,1)} %stack.2), calls=%async_computation.2 | async-start | bytes 4194304 | tf_op jit(solution)/shard_map/all_to_all | solution.py:55
  314.0 43.6 %all-to-all-start.2 = ((bf16[128,8,256]{2,1,0:T(8,128)(2,1)}), bf16[128,8,256]{2,1,0:T(8,128)(2,1)S(1)}, u32[]{:S(2)}, u32[]{:S(2)}) async-start(bf16[128,8,256]{2,1,0:T(8,128)(2,1)} %fusion.16), calls=%async_computation.3 | async-start | bytes 1048576 | tf_op jit(solution)/shard_map/all_to_all | solution.py:64
  364.2 1.0 copy-start.2
Sparse Core Ops, SparseCore 0:
  148.5 28.3 reduce-scatter.1
